TPU v7x, 256 devices: a whole 4x4x8 slice. The times are simulated.
256 devices in a mesh: tm: 64 (over z, x, core), chan: 4 (over y).
Axes of the slice: x: 4, y: 4, z: 8, core: 2. Of those that a mesh axis runs over, the one named last changes fastest.
Arguments:
- data: bfloat16 [384, 131072], P('chan', 'tm'), may hold values from 0.049804688 to 2
- motifs: bfloat16 [384, 2048], P('chan', 'tm'), may hold values from 9.727478e-05 to 0.001953125
- loadings: float32 [64, 131072], P(None, 'tm'), as said below
Outputs:
- factors_now: float32 [64, 131072], P(None, 'tm')
Inputs may be any that keep to these rules, and one draw needn't show every extreme that they name: `loadings`: every entry is positive.
All inputs are finite; a program needn't handle non-finite values.
Results may differ from a plain program's by a relative error of at most 0.0003.
Values may be sent and summed in bfloat16 or wider, within the bound.
A program may use at most 128 MiB of HBM per device.

v0:
```python
import functools

import jax
import jax.numpy as jnp
from jax import lax
from jax.experimental import pallas as pl
from jax.experimental.pallas import tpu as pltpu
from jax.sharding import PartitionSpec as P

FACTORS = 64
LAGS = 32
ITERS = 3
LANES = 128
HALO = LAGS
penalty_weight = 0.2

F32 = jnp.float32
BF16 = jnp.bfloat16
MESH = pl.DeviceIdType.MESH
NT = (((1,), (1,)), ((), ()))
TN = (((0,), (0,)), ((), ()))

NX = 4
NC = 2


def kernel(nz, ny, total, w_ref, x_ref, h_ref, out_ref, df, hst, r, r4, q, num, fa,
           halo_src, halo_l, halo_r, gsrc, cbuf, part, xbuf, ybuf, zbuf, gtot, fin,
           send_sem, recv_sem):
    own = h_ref.shape[1]
    tm = lax.axis_index("tm")
    y = lax.axis_index("chan")
    core = tm % NC
    x = (tm // NC) % NX
    z = tm // (NC * NX)
    ntm = nz * NX * NC

    def at(zz, xx, cc, yy):
        return ((zz * NX + xx) * NC + cc, yy)

    spot = tm * ny + y
    right_spot = (spot + 1) % (ntm * ny)
    left_spot = (spot + ntm * ny - 1) % (ntm * ny)
    right = (right_spot // ny, right_spot % ny)
    left = (left_spot // ny, left_spot % ny)
    first = spot == 0
    last = spot == ntm * ny - 1

    other = at(z, x, 1 - core, y)
    along_x = [at(z, (x + d) % NX, core, y) for d in range(1, NX)]
    along_y = [at(z, x, core, (y + d) % ny) for d in range(1, ny)]
    along_z = [at((z + d) % nz, x, core, y) for d in range(1, nz)]

    barrier = pltpu.get_barrier_semaphore()
    everyone = [other, left, right] + along_x + along_y + along_z
    for device in everyone:
        pl.semaphore_signal(barrier, inc=1, device_id=device, device_id_type=MESH)
    pl.semaphore_wait(barrier, len(everyone))

    count = [0]

    def remote(src, dst, device):
        slot = count[0]
        count[0] += 1
        copy = pltpu.make_async_remote_copy(
            src_ref=src, dst_ref=dst, send_sem=send_sem.at[slot], recv_sem=recv_sem.at[slot],
            device_id=device, device_id_type=MESH)
        copy.start()
        return copy

    def correlate():
        rows = own + 16
        for a in range(4):
            r4[:, 512 * a:512 * a + 512] = r[8 * a:8 * a + rows, :]
        acc = None
        for a in range(4):
            d = lax.dot_general(r4[:, 512 * a:512 * a + 512], w_ref[512 * a:512 * a + 512, :], NT,
                                preferred_element_type=F32)
            acc = d if acc is None else acc + d
        q[...] = acc
        s = q[0:own + 8, 0:LANES]
        for b in range(1, 4):
            s = s + q[2 * b:2 * b + own + 8, LANES * b:LANES * b + LANES]
        return s[0:own, 0:FACTORS] + s[1:own + 1, FACTORS:2 * FACTORS]

    def convolve():
        rows = own + HALO
        for j in range(LAGS // 2):
            hst[:, LANES * j:LANES * j + LANES] = df[HALO - 2 * j:HALO - 2 * j + rows, :].astype(BF16)
        r[0:rows, :] = jnp.dot(hst[...], w_ref[...], preferred_element_type=F32).astype(BF16)
        tail = r[own:rows, :]
        r[own:rows, :] = jnp.where(last, jnp.zeros_like(tail), tail)

    def put_field(field):
        df[HALO:HALO + own, 0:FACTORS] = field
        df[HALO + 1:HALO + own + 1, FACTORS:2 * FACTORS] = field
        hi = field.astype(BF16)
        lo = (field - hi.astype(F32)).astype(BF16)
        fa[:, 0:FACTORS] = hi
        fa[:, FACTORS:2 * FACTORS] = lo

    def put_halos(it):
        from_left = halo_l[it]
        from_left = jnp.where(first, jnp.zeros_like(from_left), from_left)
        from_right = halo_r[it]
        df[0:HALO, 0:FACTORS] = from_left
        df[1:HALO + 1, FACTORS:2 * FACTORS] = from_left
        df[HALO + own:own + 2 * HALO, 0:FACTORS] = from_right
        df[HALO + own + 1:own + 2 * HALO, FACTORS:2 * FACTORS] = from_right[0:HALO - 1]

    def send_halos(it, field):
        halo_src[it, 0] = field[0:HALO]
        halo_src[it, 1] = field[own - HALO:own]
        return [remote(halo_src.at[it, 0], halo_r.at[it], left),
                remote(halo_src.at[it, 1], halo_l.at[it], right)]

    row_id = lax.broadcasted_iota(jnp.int32, (FACTORS, FACTORS), 0)
    col_id = lax.broadcasted_iota(jnp.int32, (FACTORS, FACTORS), 1)
    off_mask = jnp.where(row_id == col_id, 0.0, penalty_weight / total).astype(F32)

    df[0:8, :] = jnp.zeros((8, 2 * FACTORS), F32)
    r[...] = x_ref[...]
    field = h_ref[...].T
    for it in range(ITERS):
        pending = send_halos(it, field)
        put_field(field)
        gg = lax.dot_general(fa[...], fa[...], TN, preferred_element_type=F32)
        gram = (gg[0:FACTORS, 0:FACTORS] + gg[0:FACTORS, FACTORS:] + gg[FACTORS:, 0:FACTORS]
                + gg[FACTORS:, FACTORS:])
        packed = jnp.concatenate([gram[0:32], gram[32:64]], axis=1)
        gsrc[it, 0] = packed[0:16]
        gsrc[it, 1] = packed[16:32]
        c0 = remote(gsrc.at[it, 1 - core], cbuf.at[it], other)
        c0.wait_recv()
        part[it, 0] = gsrc[it, core] + cbuf[it]
        cx = [remote(part.at[it, 0], xbuf.at[it, d], dev) for d, dev in enumerate(along_x)]
        if it == 0:
            num[...] = correlate()
        for c in cx:
            c.wait_recv()
        part[it, 1] = part[it, 0] + xbuf[it, 0] + xbuf[it, 1] + xbuf[it, 2]
        cy = [remote(part.at[it, 1], ybuf.at[it, d], dev) for d, dev in enumerate(along_y)]
        for c in pending:
            c.wait_recv()
        put_halos(it)
        convolve()
        for c in cy:
            c.wait_recv()
        acc = part[it, 1]
        for d in range(ny - 1):
            acc = acc + ybuf[it, d]
        part[it, 2] = acc
        cz = [remote(part.at[it, 2], zbuf.at[it, d], dev) for d, dev in enumerate(along_z)]
        denom = correlate()
        for c in cz:
            c.wait_recv()
        acc = part[it, 2]
        for d in range(nz - 1):
            acc = acc + zbuf[it, d]
        part[it, 3] = acc
        c1 = remote(part.at[it, 3], gtot.at[it], other)
        c1.wait_recv()
        mine, theirs = part[it, 3], gtot[it]
        low = jnp.where(core == 0, mine, theirs)
        high = jnp.where(core == 0, theirs, mine)
        packed = jnp.concatenate([low, high], axis=0)
        off = jnp.concatenate([packed[:, 0:FACTORS], packed[:, FACTORS:]], axis=0) * off_mask
        off_hi = off.astype(BF16)
        off_lo = (off - off_hi.astype(F32)).astype(BF16)
        penalty = (jnp.dot(fa[...], jnp.concatenate([off_hi, off_hi], axis=0), preferred_element_type=F32)
                   + jnp.dot(fa[:, 0:FACTORS], off_lo, preferred_element_type=F32))
        field = df[HALO:HALO + own, 0:FACTORS] * num[...] / (denom + penalty)
        for c in [c0, c1] + pending + cx + cy + cz:
            c.wait_send()

    fin[...] = field.T
    columns = pl.ds(pl.multiple_of(y * own, own), own)
    out_ref[:, columns] = fin[...]
    copies = [remote(fin, out_ref.at[:, columns], dev) for dev in along_y]
    for c in copies:
        c.wait()


def on_device(data, motifs, loadings):
    ntm, ny = lax.axis_size("tm"), lax.axis_size("chan")
    blocks, steps = data.shape
    own = steps // ny
    y = lax.axis_index("chan")
    pad = LANES - blocks
    piece = jnp.pad(motifs.T, ((0, 0), (0, pad)))
    everything = lax.all_gather(piece, ("chan", "tm")).reshape(ny, ntm, LAGS, LANES)
    w = jnp.transpose(everything, (2, 1, 0, 3)).reshape(LAGS * FACTORS, ny * LANES)
    pairs = [(i, i - 1) for i in range(1, ntm)]
    rim = lax.ppermute(data[:, :HALO], "tm", pairs)
    wide = jnp.concatenate([data, rim], 1)
    tiles = jnp.stack([wide[:, i * own:i * own + own + HALO] for i in range(ny)])
    tiles = lax.all_to_all(tiles, "chan", 0, 0, tiled=True)
    x = jnp.transpose(jnp.pad(tiles, ((0, 0), (0, pad), (0, 0))), (2, 0, 1)).reshape(own + HALO, ny * LANES)
    x = jnp.pad(x, ((0, 16), (0, 0)))
    mine = lax.dynamic_slice_in_dim(loadings, y * own, own, 1)

    nz = ntm // (NX * NC)
    V = pl.BlockSpec(memory_space=pltpu.VMEM)
    copies = ITERS * (4 + (NX - 1) + (ny - 1) + (nz - 1)) + (ny - 1)
    vm = pltpu.VMEM
    return pl.pallas_call(
        functools.partial(kernel, nz, ny, float(steps * ntm)),
        out_shape=jax.ShapeDtypeStruct((FACTORS, steps), F32),
        in_specs=[V, V, V],
        out_specs=V,
        scratch_shapes=[
            vm((own + 2 * HALO, 2 * FACTORS), F32),
            vm((own + HALO, LAGS * FACTORS), BF16),
            vm((own + HALO + 16, ny * LANES), BF16),
            vm((own + 16, 4 * ny * LANES), BF16),
            vm((own + 16, 4 * LANES), F32),
            vm((own, FACTORS), F32),
            vm((own, 2 * FACTORS), BF16),
            vm((ITERS, 2, HALO, FACTORS), F32),
            vm((ITERS, HALO, FACTORS), F32),
            vm((ITERS, HALO, FACTORS), F32),
            vm((ITERS, 2, 16, LANES), F32),
            vm((ITERS, 16, LANES), F32),
            vm((ITERS, 4, 16, LANES), F32),
            vm((ITERS, NX - 1, 16, LANES), F32),
            vm((ITERS, ny - 1, 16, LANES), F32),
            vm((ITERS, nz - 1, 16, LANES), F32),
            vm((ITERS, 16, LANES), F32),
            vm((FACTORS, own), F32),
            pltpu.SemaphoreType.DMA((copies,)),
            pltpu.SemaphoreType.DMA((copies,)),
        ],
        compiler_params=pltpu.CompilerParams(collective_id=0, has_side_effects=True),
    )(w, x, mine)


def solution(mesh):
    in_specs = (P("chan", "tm"), P("chan", "tm"), P(None, "tm"))
    out_specs = P(None, "tm")
    return jax.shard_map(
        on_device, mesh=mesh, in_specs=in_specs, out_specs=out_specs, check_vma=False
    )
```

profile of v0, /device:TPU:1, one launch (start us, length us, event | category | flops | bytes accessed | tf_op | source)
XLA Modules:
  0.0 193.8 jit_solution(3400532973157001578)
XLA Ops:
  6.5 0.0 copy-start
  6.5 0.0 all-gather.3.cloned.1.call-start
  6.5 1.3 pad.12
  7.9 0.0 all-gather.3.cloned.1.call-update
  7.9 0.7 slice.18
  8.7 5.1 %collective-permute-start = (bf16[96,32]{1,0:T(8,128)(2,1)S(1)}, bf16[96,32]{1,0:T(8,128)(2,1)S(1)}, u32[]{:S(2)}, u32[]{:S(2)}) collective-permute-start(bf16[96,32]{1,0:T(8,128)(2,1)S(1)} %slice.18), channel_id=1, source_target_pairs={{4,0},{8,4},{12,8},{16,12},{20,16},{24,20},{28,24},{32,28},{36,32}... | collective-permute-start | bytes 18440 | tf_op jit(solution)/shard_map/ppermute | solution.py:194
  13.8 0.9 collective-permute-done
  14.6 1.1 slice_bitcast_fusion.2
  15.8 0.9 pad_maximum_fusion
  16.6 4.2 %all-to-all-start = ((bf16[4,96,544]{2,1,0:T(8,128)(2,1)}), bf16[4,96,544]{2,1,0:T(8,128)(2,1)S(1)}, u32[]{:S(2)}, u32[]{:S(2)}) async-start(bf16[4,96,544]{2,1,0:T(8,128)(2,1)} %pad_maximum_fusion), calls=%async_computation | async-start | bytes 983040 | tf_op jit(solution)/shard_map/all_to_all | solution.py:197
  20.8 0.0 copy-done
  20.8 0.7 constant_dynamic-slice_fusion.h_ref
  21.5 9.0 %all-to-all-done = bf16[4,96,544]{2,1,0:T(8,128)(2,1)S(1)} async-done(((bf16[4,96,544]{2,1,0:T(8,128)(2,1)}), bf16[4,96,544]{2,1,0:T(8,128)(2,1)S(1)}, u32[]{:S(2)}, u32[]{:S(2)}) %all-to-all-start) | async-done | bytes 417824 | tf_op jit(solution)/shard_map/all_to_all | solution.py:197
  30.5 0.1 pad.13
  30.6 0.2 copy.6
  30.8 0.9 pad.14.x_ref
  31.7 87.7 %all-gather.3.cloned.1.call-done = bf16[8192,128]{1,0:T(8,128)(2,1)} async-done(((bf16[32,128]{1,0:T(8,128)(2,1)}), bf16[8192,128]{1,0:T(8,128)(2,1)}) %all-gather.3.cloned.1.call-update) | async-done | bytes 2097168 | tf_op jit(solution)/shard_map/all_gather | solution.py:191
  119.4 3.2 %copy.4 = bf16[4,64,32,128]{3,0,1,2:T(4,128)(2,1)S(1)} copy(bf16[4,64,32,128]{3,2,1,0:T(8,128)(2,1)} %bitcast.22) | data formatting | bytes 4194304 | tf_op jit(solution)/shard_map/reshape | solution.py:191
  122.6 1.7 copy.9
  124.3 60.8 %shard_map.37 = f32[64,2048]{1,0:T(8,128)} custom-call(bf16[2048,512]{1,0:T(8,128)(2,1)} %bitcast.19, bf16[560,512]{1,0:T(8,128)(2,1)} %pad.14.x_ref, f32[64,512]{1,0:T(8,128)} %constant_dynamic-slice_fusion.h_ref), custom_call_target="tpu_custom_call" | custom-call | tf_op jit(solution)/shard_map/pallas_call | solution.py:206
  185.1 1.9 copy.11
Async XLA Ops:
  6.5 14.3 %copy-start = (f32[64,2048]{1,0:T(8,128)S(1)}, f32[64,2048]{1,0:T(8,128)}, u32[]{:S(2)}) copy-start(f32[64,2048]{1,0:T(8,128)} %param.5) | copy-start | bytes 1572868
  6.5 112.9 %all-gather.3.cloned.1.call-start = ((), (), s32[]{:S(2)}) async-start(), calls=%async_computation.1 | async-start | bytes 2105344 | tf_op jit(solution)/shard_map/all_gather | solution.py:191
  8.7 6.0 %collective-permute-start = (bf16[96,32]{1,0:T(8,128)(2,1)S(1)}, bf16[96,32]{1,0:T(8,128)(2,1)S(1)}, u32[]{:S(2)}, u32[]{:S(2)}) collective-permute-start(bf16[96,32]{1,0:T(8,128)(2,1)S(1)} %slice.18), channel_id=1, source_target_pairs={{4,0},{8,4},{12,8},{16,12},{20,16},{24,20},{28,24},{32,28},{36,32}... | collective-permute-start | bytes 18440 | tf_op jit(solution)/shard_map/ppermute | solution.py:194
  16.6 13.9 %all-to-all-start = ((bf16[4,96,544]{2,1,0:T(8,128)(2,1)}), bf16[4,96,544]{2,1,0:T(8,128)(2,1)S(1)}, u32[]{:S(2)}, u32[]{:S(2)}) async-start(bf16[4,96,544]{2,1,0:T(8,128)(2,1)} %pad_maximum_fusion), calls=%async_computation | async-start | bytes 983040 | tf_op jit(solution)/shard_map/all_to_all | solution.py:197
Sparse Core Ops, SparseCore 0:
  11.1 108.2 all-gather.2
where the time goes:
time: 194 us
  waiting for transfers between devices  97.6 us (50%)
  Pallas kernels  60.8 us (31%)
  between operations  13.4 us (7%)
  local copies, waits for them, and re-layouts  10.7 us (6%)
  starting transfers between devices  9.28 us (5%)
  other arithmetic  1.99 us (1%)
    all_gather x1, waiting for transfers between devices, on_device(): lax.all_gather(piece, ('chan', 'tm')).reshape(ny, ntm, LAGS, LANES)  87.7 us
    pallas_call x1, Pallas kernels, on_device(): pl.pallas_call(functools.partial(kernel, nz, ny, float(steps * ntm)), out...  60.8 us
    all_to_all x1, waiting for transfers between devices, on_device(): tiles = lax.all_to_all(tiles, 'chan', 0, 0, tiled=True)  9.01 us
    ppermute x1, starting transfers between devices, on_device(): rim = lax.ppermute(data[:, :HALO], 'tm', pairs)  5.1 us
    all_to_all x1, starting transfers between devices, on_device(): tiles = lax.all_to_all(tiles, 'chan', 0, 0, tiled=True)  4.18 us
  transfers between devices with their start and end apart: 3, of which 3 were waited for; matrix products, arithmetic and copies ran while one was open for 2% of the time, Pallas kernels for 0%

commit v1 on v0

v1 whole, which is shorter than its diff:
```python
import functools

import jax
import jax.numpy as jnp
from jax import lax
from jax.experimental import pallas as pl
from jax.experimental.pallas import tpu as pltpu
from jax.sharding import PartitionSpec as P

FACTORS = 64
LAGS = 32
ITERS = 3
LANES = 128
HALO = LAGS
penalty_weight = 0.2

F32 = jnp.float32
BF16 = jnp.bfloat16
MESH = pl.DeviceIdType.MESH
NT = (((1,), (1,)), ((), ()))
TN = (((0,), (0,)), ((), ()))

NX = 4
NC = 2


def kernel(nz, ny, total, m_ref, x_ref, h_ref, out_ref, src, got, wf, w_ref, tiles, rim_src, rim,
           df, hst, r, r4, q, num, fa, halo_src, halo_l, halo_r, gsrc, cbuf, part, xybuf, zbuf, gtot,
           fin, send_sem, recv_sem):
    blocks = m_ref.shape[0]
    own = h_ref.shape[1] // ny
    tm = lax.axis_index("tm")
    y = lax.axis_index("chan")
    core = tm % NC
    x = (tm // NC) % NX
    z = tm // (NC * NX)
    ntm = nz * NX * NC

    def at(zz, xx, cc, yy):
        return ((zz * NX + xx) * NC + cc, yy)

    spot = tm * ny + y
    right_spot = (spot + 1) % (ntm * ny)
    left_spot = (spot + ntm * ny - 1) % (ntm * ny)
    right = (right_spot // ny, right_spot % ny)
    left = (left_spot // ny, left_spot % ny)
    first = spot == 0
    last = spot == ntm * ny - 1

    other = at(z, x, 1 - core, y)
    along_x = [at(z, (x + d) % NX, core, y) for d in range(1, NX)]
    along_y = [at(z, x, core, (y + d) % ny) for d in range(1, ny)]
    across = [at(z, (x + d) % NX, core, (y + e) % ny) for d in range(NX) for e in range(ny) if d or e]
    along_z = [at((z + d) % nz, x, core, y) for d in range(1, nz)]

    barrier = pltpu.get_barrier_semaphore()
    everyone = [other, left, right] + across + along_z
    for device in everyone:
        pl.semaphore_signal(barrier, inc=1, device_id=device, device_id_type=MESH)
    pl.semaphore_wait(barrier, len(everyone))

    count = [0]

    def remote(src, dst, device):
        slot = count[0]
        count[0] += 1
        copy = pltpu.make_async_remote_copy(
            src_ref=src, dst_ref=dst, send_sem=send_sem.at[slot], recv_sem=recv_sem.at[slot],
            device_id=device, device_id_type=MESH)
        copy.start()
        return copy

    def correlate():
        rows = own + 16
        for a in range(4):
            r4[:, 512 * a:512 * a + 512] = r[8 * a:8 * a + rows, :]
        acc = None
        for a in range(4):
            d = lax.dot_general(r4[:, 512 * a:512 * a + 512], w_ref[512 * a:512 * a + 512, :], NT,
                                preferred_element_type=F32)
            acc = d if acc is None else acc + d
        q[...] = acc
        s = q[0:own + 8, 0:LANES]
        for b in range(1, 4):
            s = s + q[2 * b:2 * b + own + 8, LANES * b:LANES * b + LANES]
        return s[0:own, 0:FACTORS] + s[1:own + 1, FACTORS:2 * FACTORS]

    def stack():
        for j in range(LAGS // 2):
            hst[:, LANES * j:LANES * j + LANES] = (
                df[HALO - 2 * j:HALO - 2 * j + own + HALO, :].astype(BF16))

    def convolve():
        rows = own + HALO
        r[0:rows, :] = jnp.dot(hst[...], w_ref[...], preferred_element_type=F32).astype(BF16)
        tail = r[own:rows, :]
        r[own:rows, :] = jnp.where(last, jnp.zeros_like(tail), tail)

    def put_field(field):
        df[HALO:HALO + own, 0:FACTORS] = field
        df[HALO + 1:HALO + own + 1, FACTORS:2 * FACTORS] = field
        hi = field.astype(BF16)
        lo = (field - hi.astype(F32)).astype(BF16)
        fa[:, 0:FACTORS] = hi
        fa[:, FACTORS:2 * FACTORS] = lo

    def put_halos(it):
        from_left = halo_l[it]
        from_left = jnp.where(first, jnp.zeros_like(from_left), from_left)
        from_right = halo_r[it]
        df[0:HALO, 0:FACTORS] = from_left
        df[1:HALO + 1, FACTORS:2 * FACTORS] = from_left
        df[HALO + own:own + 2 * HALO, 0:FACTORS] = from_right
        df[HALO + own + 1:own + 2 * HALO, FACTORS:2 * FACTORS] = from_right[0:HALO - 1]

    def send_halos(it, field):
        halo_src[it, 0] = field[0:HALO]
        halo_src[it, 1] = field[own - HALO:own]
        return [remote(halo_src.at[it, 0], halo_r.at[it], left),
                remote(halo_src.at[it, 1], halo_l.at[it], right)]

    row_id = lax.broadcasted_iota(jnp.int32, (FACTORS, FACTORS), 0)
    col_id = lax.broadcasted_iota(jnp.int32, (FACTORS, FACTORS), 1)
    off_mask = jnp.where(row_id == col_id, 0.0, penalty_weight / total).astype(F32)

    mine = pl.ds(pl.multiple_of(y * own, own), own)
    df[0:8, :] = jnp.zeros((8, 2 * FACTORS), F32)

    src[...] = jnp.zeros_like(src)
    src[:, 0:blocks] = m_ref[...].astype(F32).T.astype(BF16)
    pieces = [remote(src, got.at[core, y, x, z], dev) for dev in along_z]
    got[core, y, x, z] = src[...]
    sent = list(pieces)
    data = []
    for d in range(1, ny):
        there = (y + d) % ny
        columns = pl.ds(pl.multiple_of(there * own, own), own)
        data.append(remote(x_ref.at[:, columns], tiles.at[y], along_y[d - 1]))
    tiles[y] = x_ref[:, mine]
    sent += data

    def gram_start(it):
        gg = lax.dot_general(fa[...], fa[...], TN, preferred_element_type=F32)
        gram = (gg[0:FACTORS, 0:FACTORS] + gg[0:FACTORS, FACTORS:] + gg[FACTORS:, 0:FACTORS]
                + gg[FACTORS:, FACTORS:])
        packed = jnp.concatenate([gram[0:32], gram[32:64]], axis=1)
        gsrc[it, 0] = packed[0:16]
        gsrc[it, 1] = packed[16:32]
        return remote(gsrc.at[it, 1 - core], cbuf.at[it], other)

    def gram_across(it, c0):
        c0.wait_recv()
        part[it, 0] = gsrc[it, core] + cbuf[it]
        return [remote(part.at[it, 0], xybuf.at[it, d], dev) for d, dev in enumerate(across)]

    def gram_along(it, cx):
        acc = part[it, 0]
        for d, c in enumerate(cx):
            c.wait_recv()
            acc = acc + xybuf[it, d]
        part[it, 1] = acc
        return [remote(part.at[it, 1], zbuf.at[it, d], dev) for d, dev in enumerate(along_z)]

    def gram_back(it, cz):
        acc = part[it, 1]
        for d, c in enumerate(cz):
            c.wait_recv()
            acc = acc + zbuf[it, d]
        part[it, 2] = acc
        return remote(part.at[it, 2], gtot.at[it], other)

    def gram_end(it, c1):
        c1.wait_recv()
        ours, theirs = part[it, 2], gtot[it]
        low = jnp.where(core == 0, ours, theirs)
        high = jnp.where(core == 0, theirs, ours)
        packed = jnp.concatenate([low, high], axis=0)
        return jnp.concatenate([packed[:, 0:FACTORS], packed[:, FACTORS:]], axis=0) * off_mask

    def update(off, denom):
        off_hi = off.astype(BF16)
        off_lo = (off - off_hi.astype(F32)).astype(BF16)
        penalty = (jnp.dot(fa[...], jnp.concatenate([off_hi, off_hi], axis=0), preferred_element_type=F32)
                   + jnp.dot(fa[:, 0:FACTORS], off_lo, preferred_element_type=F32))
        return df[HALO:HALO + own, 0:FACTORS] * num[...] / (denom + penalty)

    field = h_ref[:, mine].T
    halos = send_halos(0, field)
    put_field(field)
    c0 = gram_start(0)
    cx = gram_across(0, c0)

    def to_partner(block):
        sent.append(remote(block, block, other))
        return sent[-1]

    for c in pieces:
        c.wait_recv()
    line = got.at[core, y, x]
    partner = [to_partner(line)]
    from_x = [remote(line, line, dev) for dev in along_x]
    from_y = [remote(line, line, dev) for dev in along_y]
    sent += from_x + from_y

    r[...] = jnp.zeros_like(r)
    for c in data:
        c.wait_recv()
    for c in range(ny):
        r[0:own, LANES * c:LANES * c + blocks] = tiles[c].astype(F32).T.astype(BF16)
    rim_src[...] = r[0:HALO, :]
    rims = [remote(rim_src, rim, left)]
    sent += rims

    cz = gram_along(0, cx)
    low_half, high_half = pl.ds(0, 16), pl.ds(16, 16)
    later = []
    for d in range(1, ny):
        from_y[d - 1].wait_recv()
        block = got.at[core, (y + ny - d) % ny, x]
        half = block.at[:, low_half, :]
        on = [remote(half, half, dev) for dev in along_x]
        later += [(c, got.at[core, (y + ny - d) % ny, (x + NX - e - 1) % NX].at[:, low_half, :])
                  for e, c in enumerate(on)]
        partner.append(to_partner(block))
    for d in range(1, NX):
        from_x[d - 1].wait_recv()
        block = got.at[core, y, (x + NX - d) % NX]
        half = block.at[:, high_half, :]
        on = [remote(half, half, dev) for dev in along_y]
        later += [(c, got.at[core, (y + ny - e - 1) % ny, (x + NX - d) % NX].at[:, high_half, :])
                  for e, c in enumerate(on)]
        partner.append(to_partner(block))
    c1 = gram_back(0, cz)
    for c in halos:
        c.wait_recv()
    put_halos(0)
    stack()
    for c in rims:
        c.wait_recv()
    tail = rim[...]
    r[own:own + HALO, :] = jnp.where(last, jnp.zeros_like(tail), tail)
    off = gram_end(0, c1)
    for c, half in later:
        c.wait_recv()
        partner.append(to_partner(half))
    sent += [c for c, _ in later]

    def spread(cc):
        def one(i, _):
            for xx in range(NX):
                for yy in range(ny):
                    wf[yy, pl.ds((i * NX + xx) * NC + cc, LAGS, stride=FACTORS), :] = (
                        got[cc, yy, xx, i].astype(F32))
            return 0

        lax.fori_loop(0, nz, one, 0)

    spread(core)
    for c in partner:
        c.wait_recv()
    spread(1 - core)

    def narrow(i, _):
        rows = pl.ds(pl.multiple_of(i * LANES, LANES), LANES)
        for yy in range(ny):
            w_ref[rows, LANES * yy:LANES * yy + LANES] = wf[yy, rows, :].astype(BF16)
        return 0

    lax.fori_loop(0, LAGS * FACTORS // LANES, narrow, 0)
    num[...] = correlate()
    convolve()
    denom = correlate()
    field = update(off, denom)
    sent += halos + [c0, c1] + cx + cz

    for it in range(1, ITERS):
        halos = send_halos(it, field)
        put_field(field)
        c0 = gram_start(it)
        cx = gram_across(it, c0)
        for c in halos:
            c.wait_recv()
        put_halos(it)
        stack()
        convolve()
        cz = gram_along(it, cx)
        denom = correlate()
        c1 = gram_back(it, cz)
        off = gram_end(it, c1)
        field = update(off, denom)
        sent += halos + [c0, c1] + cx + cz

    fin[...] = field.T
    out_ref[:, mine] = fin[...]
    copies = [remote(fin, out_ref.at[:, mine], dev) for dev in along_y]
    for c in copies:
        c.wait_recv()
    for c in sent + copies:
        c.wait_send()


def on_device(data, motifs, loadings):
    ntm, ny = lax.axis_size("tm"), lax.axis_size("chan")
    blocks, steps = data.shape
    own = steps // ny
    nz = ntm // (NX * NC)
    V = pl.BlockSpec(memory_space=pltpu.VMEM)
    copies = ITERS * (4 + NX * ny - 1 + nz - 1) + 120
    vm = pltpu.VMEM
    return pl.pallas_call(
        functools.partial(kernel, nz, ny, float(steps * ntm)),
        out_shape=jax.ShapeDtypeStruct((FACTORS, steps), F32),
        in_specs=[V, V, V],
        out_specs=V,
        scratch_shapes=[
            vm((LAGS, LANES), BF16),
            vm((NC, ny, NX, nz, LAGS, LANES), BF16),
            vm((ny, LAGS * FACTORS, LANES), F32),
            vm((LAGS * FACTORS, ny * LANES), BF16),
            vm((ny, blocks, own), BF16),
            vm((HALO, ny * LANES), BF16),
            vm((HALO, ny * LANES), BF16),
            vm((own + 2 * HALO, 2 * FACTORS), F32),
            vm((own + HALO, LAGS * FACTORS), BF16),
            vm((own + HALO + 16, ny * LANES), BF16),
            vm((own + 16, 4 * ny * LANES), BF16),
            vm((own + 16, 4 * LANES), F32),
            vm((own, FACTORS), F32),
            vm((own, 2 * FACTORS), BF16),
            vm((ITERS, 2, HALO, FACTORS), F32),
            vm((ITERS, HALO, FACTORS), F32),
            vm((ITERS, HALO, FACTORS), F32),
            vm((ITERS, 2, 16, LANES), F32),
            vm((ITERS, 16, LANES), F32),
            vm((ITERS, 4, 16, LANES), F32),
            vm((ITERS, NX * ny - 1, 16, LANES), F32),
            vm((ITERS, nz - 1, 16, LANES), F32),
            vm((ITERS, 16, LANES), F32),
            vm((FACTORS, own), F32),
            pltpu.SemaphoreType.DMA((copies,)),
            pltpu.SemaphoreType.DMA((copies,)),
        ],
        compiler_params=pltpu.CompilerParams(collective_id=0, has_side_effects=True),
    )(motifs, data, loadings)


def solution(mesh):
    in_specs = (P("chan", "tm"), P("chan", "tm"), P(None, "tm"))
    out_specs = P(None, "tm")
    return jax.shard_map(
        on_device, mesh=mesh, in_specs=in_specs, out_specs=out_specs, check_vma=False
    )
```

time: 194 us -> 77.7 us (0.40)
  waiting for transfers between devices: 97.6 us -> 0 us
  Pallas kernels: 60.8 us -> 74.2 us
  between operations: 13.4 us -> 0.01 us
  starting transfers between devices: 9.28 us -> 0 us
  local copies, waits for them, and re-layouts: 10.7 us -> 3.27 us
  other arithmetic: 1.99 us -> 0 us
    all_gather x1 -> x0, waiting for transfers between devices: 87.7 us -> none  [on_device(): lax.all_gather(piece, ('chan', 'tm')).reshape(ny, ntm, LAGS, LANES)]
    pallas_call x1, Pallas kernels: 60.8 us -> 74.2 us  [on_device(): pl.pallas_call(functools.partial(kernel, nz, ny, float(steps * ntm)), out...]
    all_to_all x1 -> x0, waiting for transfers between devices: 9.01 us -> none  [on_device(): tiles = lax.all_to_all(tiles, 'chan', 0, 0, tiled=True)]
    ppermute x1 -> x0, starting transfers between devices: 5.1 us -> none  [on_device(): rim = lax.ppermute(data[:, :HALO], 'tm', pairs)]
    all_to_all x1 -> x0, starting transfers between devices: 4.18 us -> none  [on_device(): tiles = lax.all_to_all(tiles, 'chan', 0, 0, tiled=True)]
    reshape x2 -> x0, local copies, waits for them, and re-layouts: 3.44 us -> none  [the longest x1 3.21 us: on_device(): lax.all_gather(piece, ('chan', 'tm')).reshape(ny, ntm, LAGS, LANES)]
    pad x3 -> x0, local copies, waits for them, and re-layouts: 2.26 us -> none  [the longest x1 1.35 us: on_device(): piece = jnp.pad(motifs.T, ((0, 0), (0, pad)))]
    another operation x2 -> x0, other arithmetic: 1.99 us -> none  [on_device(): jnp.stack([wide[:, i * own:i * own + own + HALO] for i in range(ny)])]
  transfers between devices with their start and end apart: 3 -> 0, of which waited for: 3 -> 0; matrix products, arithmetic and copies ran while one was open for 2% -> 0% of each run, Pallas kernels for 0% -> 0%
where the time goes in v1:
time: 77.7 us; the launch traced here: 77.5 us
  Pallas kernels  74.2 us (95%)
  local copies, waits for them, and re-layouts  3.27 us (4%)
    pallas_call x1, Pallas kernels, on_device(): pl.pallas_call(functools.partial(kernel, nz, ny, float(steps * ntm)), out...  74.2 us
    unnamed x2, local copies, waits for them, and re-layouts  3.27 us

profile of v1, /device:TPU:1, one launch (start us, length us, event | category | flops | bytes accessed | tf_op | source)
XLA Modules:
  0.0 77.5 jit_solution(10815127806814907407)
XLA Ops:
  0.0 1.4 %copy.4.m_ref = bf16[96,32]{1,0:T(8,128)(2,1)} copy(bf16[96,32]{0,1:T(8,128)(2,1)} %param.4) | data formatting | bytes 12288 | tf_op args[1]
  1.4 74.2 %shard_map.37 = f32[64,2048]{1,0:T(8,128)} custom-call(bf16[96,32]{1,0:T(8,128)(2,1)} %copy.4.m_ref, bf16[96,2048]{1,0:T(8,128)(2,1)} %x_ref.1, f32[64,2048]{1,0:T(8,128)} %h_ref.1), custom_call_target="tpu_custom_call" | custom-call | tf_op jit(solution)/shard_map/pallas_call | solution.py:310
  75.6 1.9 %copy.6 = f32[64,2048]{1,0:T(8,128)} copy(f32[64,2048]{1,0:T(8,128)} %shard_map.37) | data formatting | bytes 1048576

commit v2 on v1

--- a/solution.py
+++ b/solution.py
@@ -24,10 +24,10 @@
 NC = 2
 
 
-def kernel(nz, ny, total, m_ref, x_ref, h_ref, out_ref, src, got, wf, w_ref, tiles, rim_src, rim,
+def kernel(nz, ny, total, m_ref, x_ref, h_ref, out_ref, src, got, wf, w_ref, tiles, h_own, rim_src, rim,
            df, hst, r, r4, q, num, fa, halo_src, halo_l, halo_r, gsrc, cbuf, part, xybuf, zbuf, gtot,
-           fin, send_sem, recv_sem):
-    blocks = m_ref.shape[0]
+           fin, send_sem, recv_sem, in_sem):
+    blocks = m_ref.shape[1]
     own = h_ref.shape[1] // ny
     tm = lax.axis_index("tm")
     y = lax.axis_index("chan")
@@ -53,22 +53,37 @@
     across = [at(z, (x + d) % NX, core, (y + e) % ny) for d in range(NX) for e in range(ny) if d or e]
     along_z = [at((z + d) % nz, x, core, y) for d in range(1, nz)]
 
+    mine = pl.ds(pl.multiple_of(y * own, own), own)
+    h_in = pltpu.make_async_copy(h_ref.at[:, mine], h_own, in_sem.at[0])
+    h_in.start()
+    x_in = pltpu.make_async_copy(x_ref.at[:, mine], tiles.at[y], in_sem.at[1])
+    x_in.start()
+
     barrier = pltpu.get_barrier_semaphore()
     everyone = [other, left, right] + across + along_z
     for device in everyone:
         pl.semaphore_signal(barrier, inc=1, device_id=device, device_id_type=MESH)
+    src[...] = jnp.zeros_like(src)
+    src[:, 0:blocks] = m_ref[...]
+    df[0:8, :] = jnp.zeros((8, 2 * FACTORS), F32)
     pl.semaphore_wait(barrier, len(everyone))
 
     count = [0]
 
-    def remote(src, dst, device):
+    def remote(src, dst, device, at_slot=None):
         slot = count[0]
         count[0] += 1
         copy = pltpu.make_async_remote_copy(
-            src_ref=src, dst_ref=dst, send_sem=send_sem.at[slot], recv_sem=recv_sem.at[slot],
+            src_ref=src, dst_ref=dst, send_sem=send_sem.at[slot],
+            recv_sem=recv_sem.at[slot if at_slot is None else at_slot],
             device_id=device, device_id_type=MESH)
         copy.start()
         return copy
+
+    def arrival(block, slot):
+        pltpu.make_async_remote_copy(
+            src_ref=block, dst_ref=block, send_sem=send_sem.at[slot], recv_sem=recv_sem.at[slot],
+            device_id=other, device_id_type=MESH).wait_recv()
 
     def correlate():
         rows = own + 16
@@ -99,6 +114,8 @@
     def put_field(field):
         df[HALO:HALO + own, 0:FACTORS] = field
         df[HALO + 1:HALO + own + 1, FACTORS:2 * FACTORS] = field
+
+    def put_gram(field):
         hi = field.astype(BF16)
         lo = (field - hi.astype(F32)).astype(BF16)
         fa[:, 0:FACTORS] = hi
@@ -123,20 +140,22 @@
     col_id = lax.broadcasted_iota(jnp.int32, (FACTORS, FACTORS), 1)
     off_mask = jnp.where(row_id == col_id, 0.0, penalty_weight / total).astype(F32)
 
-    mine = pl.ds(pl.multiple_of(y * own, own), own)
-    df[0:8, :] = jnp.zeros((8, 2 * FACTORS), F32)
-
-    src[...] = jnp.zeros_like(src)
-    src[:, 0:blocks] = m_ref[...].astype(F32).T.astype(BF16)
-    pieces = [remote(src, got.at[core, y, x, z], dev) for dev in along_z]
     got[core, y, x, z] = src[...]
-    sent = list(pieces)
+    pairs = nz // 2
+    pair = z // 2
+    base = count[0]
+    count[0] += pairs
+    piece = got.at[core, y, x, z]
+    sent = [remote(src, piece, at(pair * 2 + 1 - z % 2, x, core, y), base)]
+    for p in [1, pairs - 1] + list(range(2, pairs - 1)):
+        for b in range(2):
+            there = (pair + pairs - p) % pairs * 2 + b
+            sent.append(remote(src, piece, at(there, x, core, y), base + p))
     data = []
     for d in range(1, ny):
         there = (y + d) % ny
         columns = pl.ds(pl.multiple_of(there * own, own), own)
         data.append(remote(x_ref.at[:, columns], tiles.at[y], along_y[d - 1]))
-    tiles[y] = x_ref[:, mine]
     sent += data
 
     def gram_start(it):
@@ -184,25 +203,50 @@
                    + jnp.dot(fa[:, 0:FACTORS], off_lo, preferred_element_type=F32))
         return df[HALO:HALO + own, 0:FACTORS] * num[...] / (denom + penalty)
 
-    field = h_ref[:, mine].T
+    def to_partner(block):
+        copy = remote(block, block, other)
+        sent.append(copy)
+        return copy
+
+    def spread(cc, yy, xx):
+        def one(i, _):
+            k = (i * NX + xx) * NC + cc
+            wf[yy, pl.ds(k, LAGS, stride=FACTORS), :] = got[cc, yy, xx, i].astype(F32)
+            return 0
+
+        lax.fori_loop(0, nz, one, 0, unroll=True)
+
+    h_in.wait()
+    field = h_own[...].T
+    put_gram(field)
+    c0 = gram_start(0)
     halos = send_halos(0, field)
+
+    order = [0, 1, pairs - 1] + list(range(2, pairs - 1))
+    low_half, high_half = pl.ds(0, 16), pl.ds(16, 16)
+
+    def zs(p):
+        return pl.ds((pair + p) % pairs * 2, 2)
+
+    from_x, from_y = {}, {}
+    for p in order:
+        if p == 0:
+            arrival(got.at[core, y, x, pair * 2 + 1 - z % 2], base)
+        else:
+            arrival(got.at[core, y, x, zs(p)], base + p)
+        block = got.at[core, y, x, zs(p)]
+        for d in (1, ny - 1, 2):
+            from_y[p, d] = remote(block, block, along_y[d - 1])
+        for d in (1, NX - 1, 2):
+            from_x[p, d] = remote(block, block, along_x[d - 1])
+        if p == 0:
+            cx = gram_across(0, c0)
+    partner = [(to_partner(got.at[core, y, x]), y, x)]
+    sent += list(from_x.values()) + list(from_y.values())
     put_field(field)
-    c0 = gram_start(0)
-    cx = gram_across(0, c0)
-
-    def to_partner(block):
-        sent.append(remote(block, block, other))
-        return sent[-1]
-
-    for c in pieces:
-        c.wait_recv()
-    line = got.at[core, y, x]
-    partner = [to_partner(line)]
-    from_x = [remote(line, line, dev) for dev in along_x]
-    from_y = [remote(line, line, dev) for dev in along_y]
-    sent += from_x + from_y
 
     r[...] = jnp.zeros_like(r)
+    x_in.wait()
     for c in data:
         c.wait_recv()
     for c in range(ny):
@@ -211,25 +255,25 @@
     rims = [remote(rim_src, rim, left)]
     sent += rims
 
-    cz = gram_along(0, cx)
-    low_half, high_half = pl.ds(0, 16), pl.ds(16, 16)
-    later = []
-    for d in range(1, ny):
-        from_y[d - 1].wait_recv()
-        block = got.at[core, (y + ny - d) % ny, x]
-        half = block.at[:, low_half, :]
-        on = [remote(half, half, dev) for dev in along_x]
-        later += [(c, got.at[core, (y + ny - d) % ny, (x + NX - e - 1) % NX].at[:, low_half, :])
-                  for e, c in enumerate(on)]
-        partner.append(to_partner(block))
+    later = {}
+    for p in order:
+        for d in (1, 3, 2):
+            yy, xx = (y + ny - d) % ny, (x + NX - d) % NX
+            from_y[p, d].wait_recv()
+            half = got.at[core, yy, x, zs(p), low_half]
+            for e in (1, 3, 2):
+                later.setdefault((d, e), []).append(remote(half, half, along_x[e - 1]))
+            from_x[p, d].wait_recv()
+            half = got.at[core, y, xx, zs(p), high_half]
+            for e in (1, 3, 2):
+                later.setdefault((e, d), []).append(remote(half, half, along_y[e - 1]))
+        if p == order[0]:
+            cz = gram_along(0, cx)
+    lines = []
     for d in range(1, NX):
-        from_x[d - 1].wait_recv()
-        block = got.at[core, y, (x + NX - d) % NX]
-        half = block.at[:, high_half, :]
-        on = [remote(half, half, dev) for dev in along_y]
-        later += [(c, got.at[core, (y + ny - e - 1) % ny, (x + NX - d) % NX].at[:, high_half, :])
-                  for e, c in enumerate(on)]
-        partner.append(to_partner(block))
+        yy, xx = (y + ny - d) % ny, (x + NX - d) % NX
+        lines += [(yy, x), (y, xx)]
+    partner += [(to_partner(got.at[core, yy, xx]), yy, xx) for yy, xx in lines]
     c1 = gram_back(0, cz)
     for c in halos:
         c.wait_recv()
@@ -239,26 +283,24 @@
         c.wait_recv()
     tail = rim[...]
     r[own:own + HALO, :] = jnp.where(last, jnp.zeros_like(tail), tail)
+    spread(core, y, x)
+    for yy, xx in lines:
+        spread(core, yy, xx)
+    early, partner = partner, []
+    for c, yy, xx in early:
+        c.wait_recv()
+        spread(1 - core, yy, xx)
+    for (d, e), copies in later.items():
+        for c in copies:
+            c.wait_recv()
+        yy, xx = (y + ny - d) % ny, (x + NX - e) % NX
+        partner.append((to_partner(got.at[core, yy, xx]), yy, xx))
+        spread(core, yy, xx)
+        sent += copies
     off = gram_end(0, c1)
-    for c, half in later:
-        c.wait_recv()
-        partner.append(to_partner(half))
-    sent += [c for c, _ in later]
-
-    def spread(cc):
-        def one(i, _):
-            for xx in range(NX):
-                for yy in range(ny):
-                    wf[yy, pl.ds((i * NX + xx) * NC + cc, LAGS, stride=FACTORS), :] = (
-                        got[cc, yy, xx, i].astype(F32))
-            return 0
-
-        lax.fori_loop(0, nz, one, 0)
-
-    spread(core)
-    for c in partner:
-        c.wait_recv()
-    spread(1 - core)
+    for c, yy, xx in partner:
+        c.wait_recv()
+        spread(1 - core, yy, xx)
 
     def narrow(i, _):
         rows = pl.ds(pl.multiple_of(i * LANES, LANES), LANES)
@@ -274,9 +316,10 @@
     sent += halos + [c0, c1] + cx + cz
 
     for it in range(1, ITERS):
+        put_gram(field)
+        c0 = gram_start(it)
         halos = send_halos(it, field)
         put_field(field)
-        c0 = gram_start(it)
         cx = gram_across(it, c0)
         for c in halos:
             c.wait_recv()
@@ -305,12 +348,13 @@
     own = steps // ny
     nz = ntm // (NX * NC)
     V = pl.BlockSpec(memory_space=pltpu.VMEM)
-    copies = ITERS * (4 + NX * ny - 1 + nz - 1) + 120
+    A = pl.BlockSpec(memory_space=pl.ANY)
+    copies = ITERS * (4 + NX * ny - 1 + nz - 1) + 160
     vm = pltpu.VMEM
     return pl.pallas_call(
         functools.partial(kernel, nz, ny, float(steps * ntm)),
         out_shape=jax.ShapeDtypeStruct((FACTORS, steps), F32),
-        in_specs=[V, V, V],
+        in_specs=[V, A, A],
         out_specs=V,
         scratch_shapes=[
             vm((LAGS, LANES), BF16),
@@ -318,6 +362,7 @@
             vm((ny, LAGS * FACTORS, LANES), F32),
             vm((LAGS * FACTORS, ny * LANES), BF16),
             vm((ny, blocks, own), BF16),
+            vm((FACTORS, own), F32),
             vm((HALO, ny * LANES), BF16),
             vm((HALO, ny * LANES), BF16),
             vm((own + 2 * HALO, 2 * FACTORS), F32),
@@ -339,9 +384,10 @@
             vm((FACTORS, own), F32),
             pltpu.SemaphoreType.DMA((copies,)),
             pltpu.SemaphoreType.DMA((copies,)),
+            pltpu.SemaphoreType.DMA((2,)),
         ],
         compiler_params=pltpu.CompilerParams(collective_id=0, has_side_effects=True),
-    )(motifs, data, loadings)
+    )(motifs.T, data, loadings)
 
 
 def solution(mesh):

time: 77.7 us -> 76.9 us (0.990)
  local copies, waits for them, and re-layouts: 3.27 us -> 1.87 us
    unnamed x2 -> x1, local copies, waits for them, and re-layouts: 3.27 us -> 1.87 us
where the time goes in v2:
time: 76.9 us; the launch traced here: 76.7 us
  Pallas kernels  74.8 us (97%)
  local copies, waits for them, and re-layouts  1.87 us (2%)
    pallas_call x1, Pallas kernels, on_device(): pl.pallas_call(functools.partial(kernel, nz, ny, float(steps * ntm)), out...  74.8 us
    unnamed x1, local copies, waits for them, and re-layouts  1.87 us

profile of v2, /device:TPU:1, one launch (start us, length us, event | category | flops | bytes accessed | tf_op | source)
XLA Modules:
  0.0 76.7 jit_solution(7470471921456131026)
XLA Ops:
  0.0 74.8 %shard_map.37 = f32[64,2048]{1,0:T(8,128)} custom-call(bf16[32,96]{1,0:T(8,128)(2,1)} %bitcast.1, bf16[96,2048]{1,0:T(8,128)(2,1)} %x_ref.1, f32[64,2048]{1,0:T(8,128)} %h_ref.1), custom_call_target="tpu_custom_call" | custom-call | tf_op jit(solution)/shard_map/pallas_call | solution.py:354
  74.9 1.9 %copy.5 = f32[64,2048]{1,0:T(8,128)} copy(f32[64,2048]{1,0:T(8,128)} %shard_map.37) | data formatting | bytes 1048576

commit v3 on v2

--- a/solution.py
+++ b/solution.py
@@ -26,7 +26,7 @@
 
 def kernel(nz, ny, total, m_ref, x_ref, h_ref, out_ref, src, got, wf, w_ref, tiles, h_own, rim_src, rim,
            df, hst, r, r4, q, num, fa, halo_src, halo_l, halo_r, gsrc, cbuf, part, xybuf, zbuf, gtot,
-           fin, send_sem, recv_sem, in_sem):
+           all_n, all_f, all_d, all_a, fb, send_sem, recv_sem, in_sem):
     blocks = m_ref.shape[1]
     own = h_ref.shape[1] // ny
     tm = lax.axis_index("tm")
@@ -169,28 +169,25 @@
 
     def gram_across(it, c0):
         c0.wait_recv()
-        part[it, 0] = gsrc[it, core] + cbuf[it]
-        return [remote(part.at[it, 0], xybuf.at[it, d], dev) for d, dev in enumerate(across)]
+        spot = x * ny + y
+        xybuf[it, spot] = gsrc[it, core] + cbuf[it]
+        return [remote(xybuf.at[it, spot], xybuf.at[it, spot], dev) for dev in across]
 
     def gram_along(it, cx):
-        acc = part[it, 0]
-        for d, c in enumerate(cx):
+        for c in cx:
             c.wait_recv()
-            acc = acc + xybuf[it, d]
-        part[it, 1] = acc
-        return [remote(part.at[it, 1], zbuf.at[it, d], dev) for d, dev in enumerate(along_z)]
+        zbuf[it, z] = sum(xybuf[it, i] for i in range(NX * ny))
+        return [remote(zbuf.at[it, z], zbuf.at[it, z], dev) for dev in along_z]
 
     def gram_back(it, cz):
-        acc = part[it, 1]
-        for d, c in enumerate(cz):
+        for c in cz:
             c.wait_recv()
-            acc = acc + zbuf[it, d]
-        part[it, 2] = acc
-        return remote(part.at[it, 2], gtot.at[it], other)
+        part[it] = sum(zbuf[it, i] for i in range(nz))
+        return remote(part.at[it], gtot.at[it], other)
 
     def gram_end(it, c1):
         c1.wait_recv()
-        ours, theirs = part[it, 2], gtot[it]
+        ours, theirs = part[it], gtot[it]
         low = jnp.where(core == 0, ours, theirs)
         high = jnp.where(core == 0, theirs, ours)
         packed = jnp.concatenate([low, high], axis=0)
@@ -260,10 +257,12 @@
         for d in (1, 3, 2):
             yy, xx = (y + ny - d) % ny, (x + NX - d) % NX
             from_y[p, d].wait_recv()
-            half = got.at[core, yy, x, zs(p), low_half]
+            half = got.at[core, yy, x, zs(p)] if p in order[:2] else got.at[core, yy, x, zs(p), low_half]
             for e in (1, 3, 2):
                 later.setdefault((d, e), []).append(remote(half, half, along_x[e - 1]))
             from_x[p, d].wait_recv()
+            if p in order[:2]:
+                continue
             half = got.at[core, y, xx, zs(p), high_half]
             for e in (1, 3, 2):
                 later.setdefault((e, d), []).append(remote(half, half, along_y[e - 1]))
@@ -315,30 +314,57 @@
     field = update(off, denom)
     sent += halos + [c0, c1] + cx + cz
 
+    def to_all_blocks(value, everyone_has):
+        everyone_has[y] = value.T
+        copies = [remote(everyone_has.at[y], everyone_has.at[y], dev) for dev in along_y]
+        sent.extend(copies)
+        return copies
+
     for it in range(1, ITERS):
         put_gram(field)
         c0 = gram_start(it)
         halos = send_halos(it, field)
         put_field(field)
         cx = gram_across(it, c0)
+        if it == ITERS - 1:
+            f_in = to_all_blocks(field, all_f)
         for c in halos:
             c.wait_recv()
         put_halos(it)
         stack()
         convolve()
-        cz = gram_along(it, cx)
+        if it < ITERS - 1:
+            cz = gram_along(it, cx)
         denom = correlate()
+        if it == ITERS - 1:
+            d_in = to_all_blocks(denom, all_d)
+            cz = gram_along(it, cx)
+            for c in n_in + f_in:
+                c.wait_recv()
+            for yy in range(ny):
+                f = all_f[yy]
+                hi = f.astype(BF16)
+                fb[yy, 0:FACTORS, :] = hi
+                fb[yy, FACTORS:2 * FACTORS, :] = (f - hi.astype(F32)).astype(BF16)
+                all_a[yy] = f * all_n[yy]
+        elif it == 1:
+            n_in = to_all_blocks(num[...], all_n)
         c1 = gram_back(it, cz)
         off = gram_end(it, c1)
-        field = update(off, denom)
+        if it < ITERS - 1:
+            field = update(off, denom)
         sent += halos + [c0, c1] + cx + cz
 
-    fin[...] = field.T
-    out_ref[:, mine] = fin[...]
-    copies = [remote(fin, out_ref.at[:, mine], dev) for dev in along_y]
-    for c in copies:
-        c.wait_recv()
-    for c in sent + copies:
+    off_hi = off.astype(BF16)
+    off_lo = (off - off_hi.astype(F32)).astype(BF16)
+    twice = jnp.concatenate([off_hi, off_hi], axis=1)
+    for c in d_in:
+        c.wait_recv()
+    for yy in range(ny):
+        penalty = (jnp.dot(twice, fb[yy], preferred_element_type=F32)
+                   + jnp.dot(off_lo, fb[yy, 0:FACTORS, :], preferred_element_type=F32))
+        out_ref[:, own * yy:own * yy + own] = all_a[yy] / (all_d[yy] + penalty)
+    for c in sent:
         c.wait_send()
 
 
@@ -377,11 +403,15 @@
             vm((ITERS, HALO, FACTORS), F32),
             vm((ITERS, 2, 16, LANES), F32),
             vm((ITERS, 16, LANES), F32),
-            vm((ITERS, 4, 16, LANES), F32),
-            vm((ITERS, NX * ny - 1, 16, LANES), F32),
-            vm((ITERS, nz - 1, 16, LANES), F32),
             vm((ITERS, 16, LANES), F32),
-            vm((FACTORS, own), F32),
+            vm((ITERS, NX * ny, 16, LANES), F32),
+            vm((ITERS, nz, 16, LANES), F32),
+            vm((ITERS, 16, LANES), F32),
+            vm((ny, FACTORS, own), F32),
+            vm((ny, FACTORS, own), F32),
+            vm((ny, FACTORS, own), F32),
+            vm((ny, FACTORS, own), F32),
+            vm((ny, 2 * FACTORS, own), BF16),
             pltpu.SemaphoreType.DMA((copies,)),
             pltpu.SemaphoreType.DMA((copies,)),
             pltpu.SemaphoreType.DMA((2,)),

time: 76.9 us -> 71.9 us (0.935)
  Pallas kernels: 74.8 us -> 69.8 us
    pallas_call x1, Pallas kernels: 74.8 us -> 69.8 us  [on_device(): pl.pallas_call(functools.partial(kernel, nz, ny, float(steps * ntm)), out...]
where the time goes in v3:
time: 71.9 us; the launch traced here: 71.7 us
  Pallas kernels  69.8 us (97%)
  local copies, waits for them, and re-layouts  1.87 us (3%)
    pallas_call x1, Pallas kernels, on_device(): pl.pallas_call(functools.partial(kernel, nz, ny, float(steps * ntm)), out...  69.8 us
    unnamed x1, local copies, waits for them, and re-layouts  1.87 us

profile of v3, /device:TPU:1, one launch (start us, length us, event | category | flops | bytes accessed | tf_op | source)
XLA Modules:
  0.0 71.7 jit_solution(11322065318321875769)
XLA Ops:
  0.0 69.8 %shard_map.37 = f32[64,2048]{1,0:T(8,128)} custom-call(bf16[32,96]{1,0:T(8,128)(2,1)} %bitcast.1, bf16[96,2048]{1,0:T(8,128)(2,1)} %x_ref.1, f32[64,2048]{1,0:T(8,128)} %h_ref.1), custom_call_target="tpu_custom_call" | custom-call | tf_op jit(solution)/shard_map/pallas_call | solution.py:380
  69.9 1.9 %copy.5 = f32[64,2048]{1,0:T(8,128)} copy(f32[64,2048]{1,0:T(8,128)} %shard_map.37) | data formatting | bytes 1048576

commit v4 on v3

--- a/solution.py
+++ b/solution.py
@@ -12,6 +12,7 @@
 ITERS = 3
 LANES = 128
 HALO = LAGS
+SLOTS = 84
 penalty_weight = 0.2
 
 F32 = jnp.float32
@@ -26,7 +27,7 @@
 
 def kernel(nz, ny, total, m_ref, x_ref, h_ref, out_ref, src, got, wf, w_ref, tiles, h_own, rim_src, rim,
            df, hst, r, r4, q, num, fa, halo_src, halo_l, halo_r, gsrc, cbuf, part, xybuf, zbuf, gtot,
-           all_n, all_f, all_d, all_a, fb, send_sem, recv_sem, in_sem):
+           all_n, all_f, all_d, all_a, fb, sem, in_sem):
     blocks = m_ref.shape[1]
     own = h_ref.shape[1] // ny
     tm = lax.axis_index("tm")
@@ -70,20 +71,23 @@
 
     count = [0]
 
-    def remote(src, dst, device, at_slot=None):
-        slot = count[0]
+    def slot():
         count[0] += 1
-        copy = pltpu.make_async_remote_copy(
-            src_ref=src, dst_ref=dst, send_sem=send_sem.at[slot],
-            recv_sem=recv_sem.at[slot if at_slot is None else at_slot],
+        return count[0] - 1
+
+    def copy_of(src, dst, device, send, recv):
+        return pltpu.make_async_remote_copy(
+            src_ref=src, dst_ref=dst, send_sem=sem.at[send], recv_sem=sem.at[recv],
             device_id=device, device_id_type=MESH)
-        copy.start()
-        return copy
-
-    def arrival(block, slot):
-        pltpu.make_async_remote_copy(
-            src_ref=block, dst_ref=block, send_sem=send_sem.at[slot], recv_sem=recv_sem.at[slot],
-            device_id=other, device_id_type=MESH).wait_recv()
+
+    def remote(src, dst, device, send, recv):
+        copy_of(src, dst, device, send, recv).start()
+
+    def arrival(block, recv):
+        copy_of(block, block, other, recv, recv).wait_recv()
+
+    def departure(block, send):
+        copy_of(block, block, other, send, send).wait_send()
 
     def correlate():
         rows = own + 16
@@ -133,8 +137,14 @@
     def send_halos(it, field):
         halo_src[it, 0] = field[0:HALO]
         halo_src[it, 1] = field[own - HALO:own]
-        return [remote(halo_src.at[it, 0], halo_r.at[it], left),
-                remote(halo_src.at[it, 1], halo_l.at[it], right)]
+        slots = (slot(), slot(), slot())
+        remote(halo_src.at[it, 0], halo_r.at[it], left, slots[0], slots[1])
+        remote(halo_src.at[it, 1], halo_l.at[it], right, slots[0], slots[2])
+        return slots
+
+    def halos_here(it, slots):
+        arrival(halo_r.at[it], slots[1])
+        arrival(halo_l.at[it], slots[2])
 
     row_id = lax.broadcasted_iota(jnp.int32, (FACTORS, FACTORS), 0)
     col_id = lax.broadcasted_iota(jnp.int32, (FACTORS, FACTORS), 1)
@@ -143,20 +153,19 @@
     got[core, y, x, z] = src[...]
     pairs = nz // 2
     pair = z // 2
-    base = count[0]
-    count[0] += pairs
+    base = [slot() for _ in range(pairs)]
     piece = got.at[core, y, x, z]
-    sent = [remote(src, piece, at(pair * 2 + 1 - z % 2, x, core, y), base)]
+    piece_send = slot()
+    remote(src, piece, at(pair * 2 + 1 - z % 2, x, core, y), piece_send, base[0])
     for p in [1, pairs - 1] + list(range(2, pairs - 1)):
         for b in range(2):
             there = (pair + pairs - p) % pairs * 2 + b
-            sent.append(remote(src, piece, at(there, x, core, y), base + p))
-    data = []
+            remote(src, piece, at(there, x, core, y), piece_send, base[p])
+    data_send, data_recv = slot(), slot()
     for d in range(1, ny):
         there = (y + d) % ny
         columns = pl.ds(pl.multiple_of(there * own, own), own)
-        data.append(remote(x_ref.at[:, columns], tiles.at[y], along_y[d - 1]))
-    sent += data
+        remote(x_ref.at[:, columns], tiles.at[y], along_y[d - 1], data_send, data_recv)
 
     def gram_start(it):
         gg = lax.dot_general(fa[...], fa[...], TN, preferred_element_type=F32)
@@ -165,28 +174,36 @@
         packed = jnp.concatenate([gram[0:32], gram[32:64]], axis=1)
         gsrc[it, 0] = packed[0:16]
         gsrc[it, 1] = packed[16:32]
-        return remote(gsrc.at[it, 1 - core], cbuf.at[it], other)
-
-    def gram_across(it, c0):
-        c0.wait_recv()
+        slots = [slot() for _ in range(8)]
+        remote(gsrc.at[it, 1 - core], cbuf.at[it], other, slots[0], slots[1])
+        return slots
+
+    def gram_across(it, slots):
+        arrival(cbuf.at[it], slots[1])
         spot = x * ny + y
         xybuf[it, spot] = gsrc[it, core] + cbuf[it]
-        return [remote(xybuf.at[it, spot], xybuf.at[it, spot], dev) for dev in across]
-
-    def gram_along(it, cx):
-        for c in cx:
-            c.wait_recv()
+        for dev in across:
+            remote(xybuf.at[it, spot], xybuf.at[it, spot], dev, slots[2], slots[3])
+
+    def gram_along(it, slots):
+        arrival(xybuf.at[it, pl.ds(0, NX * ny - 1)], slots[3])
         zbuf[it, z] = sum(xybuf[it, i] for i in range(NX * ny))
-        return [remote(zbuf.at[it, z], zbuf.at[it, z], dev) for dev in along_z]
-
-    def gram_back(it, cz):
-        for c in cz:
-            c.wait_recv()
+        for dev in along_z:
+            remote(zbuf.at[it, z], zbuf.at[it, z], dev, slots[4], slots[5])
+
+    def gram_back(it, slots):
+        arrival(zbuf.at[it, pl.ds(0, nz - 1)], slots[5])
         part[it] = sum(zbuf[it, i] for i in range(nz))
-        return remote(part.at[it], gtot.at[it], other)
-
-    def gram_end(it, c1):
-        c1.wait_recv()
+        remote(part.at[it], gtot.at[it], other, slots[6], slots[7])
+
+    def gram_sent(it, slots):
+        departure(gsrc.at[it, 0], slots[0])
+        departure(xybuf.at[it, pl.ds(0, NX * ny - 1)], slots[2])
+        departure(zbuf.at[it, pl.ds(0, nz - 1)], slots[4])
+        departure(part.at[it], slots[6])
+
+    def gram_end(it, slots):
+        arrival(gtot.at[it], slots[7])
         ours, theirs = part[it], gtot[it]
         low = jnp.where(core == 0, ours, theirs)
         high = jnp.where(core == 0, theirs, ours)
@@ -200,10 +217,17 @@
                    + jnp.dot(fa[:, 0:FACTORS], off_lo, preferred_element_type=F32))
         return df[HALO:HALO + own, 0:FACTORS] * num[...] / (denom + penalty)
 
-    def to_partner(block):
-        copy = remote(block, block, other)
-        sent.append(copy)
-        return copy
+    partner_send = slot()
+
+    def to_partner(yy, xx):
+        here = slot()
+        block = got.at[core, yy, xx]
+        remote(block, block, other, partner_send, here)
+        return yy, xx, here
+
+    def from_partner(yy, xx, here):
+        arrival(got.at[1 - core, yy, xx], here)
+        spread(1 - core, yy, xx)
 
     def spread(cc, yy, xx):
         def one(i, _):
@@ -216,90 +240,85 @@
     h_in.wait()
     field = h_own[...].T
     put_gram(field)
-    c0 = gram_start(0)
-    halos = send_halos(0, field)
+    gram_slots = gram_start(0)
+    halo_slots = send_halos(0, field)
 
     order = [0, 1, pairs - 1] + list(range(2, pairs - 1))
     low_half, high_half = pl.ds(0, 16), pl.ds(16, 16)
+    near_first = (1, 3, 2)
 
     def zs(p):
         return pl.ds((pair + p) % pairs * 2, 2)
 
-    from_x, from_y = {}, {}
+    line_send = slot()
+    from_x = [slot() for _ in range(pairs)]
+    from_y = [slot() for _ in range(pairs)]
     for p in order:
         if p == 0:
-            arrival(got.at[core, y, x, pair * 2 + 1 - z % 2], base)
+            arrival(got.at[core, y, x, pair * 2 + 1 - z % 2], base[0])
         else:
-            arrival(got.at[core, y, x, zs(p)], base + p)
+            arrival(got.at[core, y, x, zs(p)], base[p])
         block = got.at[core, y, x, zs(p)]
-        for d in (1, ny - 1, 2):
-            from_y[p, d] = remote(block, block, along_y[d - 1])
-        for d in (1, NX - 1, 2):
-            from_x[p, d] = remote(block, block, along_x[d - 1])
+        for d in near_first:
+            remote(block, block, along_y[d - 1], line_send, from_y[p])
+        for d in near_first:
+            remote(block, block, along_x[d - 1], line_send, from_x[p])
         if p == 0:
-            cx = gram_across(0, c0)
-    partner = [(to_partner(got.at[core, y, x]), y, x)]
-    sent += list(from_x.values()) + list(from_y.values())
+            gram_across(0, gram_slots)
+    early = [to_partner(y, x)]
     put_field(field)
 
     r[...] = jnp.zeros_like(r)
     x_in.wait()
-    for c in data:
-        c.wait_recv()
+    arrival(tiles.at[pl.ds(0, ny - 1)], data_recv)
     for c in range(ny):
         r[0:own, LANES * c:LANES * c + blocks] = tiles[c].astype(F32).T.astype(BF16)
     rim_src[...] = r[0:HALO, :]
-    rims = [remote(rim_src, rim, left)]
-    sent += rims
-
-    later = {}
+    rim_send, rim_recv = slot(), slot()
+    remote(rim_src, rim, left, rim_send, rim_recv)
+
+    later_send = slot()
+    later = {(d, e): slot() for d in range(1, ny) for e in range(1, NX)}
     for p in order:
-        for d in (1, 3, 2):
-            yy, xx = (y + ny - d) % ny, (x + NX - d) % NX
-            from_y[p, d].wait_recv()
-            half = got.at[core, yy, x, zs(p)] if p in order[:2] else got.at[core, yy, x, zs(p), low_half]
-            for e in (1, 3, 2):
-                later.setdefault((d, e), []).append(remote(half, half, along_x[e - 1]))
-            from_x[p, d].wait_recv()
-            if p in order[:2]:
-                continue
-            half = got.at[core, y, xx, zs(p), high_half]
-            for e in (1, 3, 2):
-                later.setdefault((e, d), []).append(remote(half, half, along_y[e - 1]))
+        whole = p in order[:2]
+        arrival(got.at[core, pl.ds(0, ny - 1), 0, pl.ds(0, 2)], from_y[p])
+        for d in near_first:
+            part_of = got.at[core, (y + ny - d) % ny, x, zs(p)]
+            if not whole:
+                part_of = got.at[core, (y + ny - d) % ny, x, zs(p), low_half]
+            for e in near_first:
+                remote(part_of, part_of, along_x[e - 1], later_send, later[d, e])
+        arrival(got.at[core, 0, pl.ds(0, NX - 1), pl.ds(0, 2)], from_x[p])
+        if not whole:
+            for d in near_first:
+                part_of = got.at[core, y, (x + NX - d) % NX, zs(p), high_half]
+                for e in near_first:
+                    remote(part_of, part_of, along_y[e - 1], later_send, later[e, d])
         if p == order[0]:
-            cz = gram_along(0, cx)
-    lines = []
+            gram_along(0, gram_slots)
     for d in range(1, NX):
         yy, xx = (y + ny - d) % ny, (x + NX - d) % NX
-        lines += [(yy, x), (y, xx)]
-    partner += [(to_partner(got.at[core, yy, xx]), yy, xx) for yy, xx in lines]
-    c1 = gram_back(0, cz)
-    for c in halos:
-        c.wait_recv()
+        early += [to_partner(yy, x), to_partner(y, xx)]
+    gram_back(0, gram_slots)
+    halos_here(0, halo_slots)
     put_halos(0)
     stack()
-    for c in rims:
-        c.wait_recv()
+    arrival(rim, rim_recv)
     tail = rim[...]
     r[own:own + HALO, :] = jnp.where(last, jnp.zeros_like(tail), tail)
-    spread(core, y, x)
-    for yy, xx in lines:
+    for yy, xx, _ in early:
         spread(core, yy, xx)
-    early, partner = partner, []
-    for c, yy, xx in early:
-        c.wait_recv()
-        spread(1 - core, yy, xx)
-    for (d, e), copies in later.items():
-        for c in copies:
-            c.wait_recv()
+    for entry in early:
+        from_partner(*entry)
+    late = []
+    for (d, e), here in later.items():
         yy, xx = (y + ny - d) % ny, (x + NX - e) % NX
-        partner.append((to_partner(got.at[core, yy, xx]), yy, xx))
+        arrival(got.at[core, yy, xx], here)
+        late.append(to_partner(yy, xx))
         spread(core, yy, xx)
-        sent += copies
-    off = gram_end(0, c1)
-    for c, yy, xx in partner:
-        c.wait_recv()
-        spread(1 - core, yy, xx)
+    off = gram_end(0, gram_slots)
+    for entry in late:
+        from_partner(*entry)
 
     def narrow(i, _):
         rows = pl.ds(pl.multiple_of(i * LANES, LANES), LANES)
@@ -312,35 +331,43 @@
     convolve()
     denom = correlate()
     field = update(off, denom)
-    sent += halos + [c0, c1] + cx + cz
 
     def to_all_blocks(value, everyone_has):
         everyone_has[y] = value.T
-        copies = [remote(everyone_has.at[y], everyone_has.at[y], dev) for dev in along_y]
-        sent.extend(copies)
-        return copies
+        slots = (slot(), slot())
+        for dev in along_y:
+            remote(everyone_has.at[y], everyone_has.at[y], dev, *slots)
+        return slots
 
     for it in range(1, ITERS):
         put_gram(field)
-        c0 = gram_start(it)
-        halos = send_halos(it, field)
+        before = gram_slots, halo_slots
+        gram_slots = gram_start(it)
+        halo_slots = send_halos(it, field)
         put_field(field)
-        cx = gram_across(it, c0)
+        gram_across(it, gram_slots)
         if it == ITERS - 1:
-            f_in = to_all_blocks(field, all_f)
-        for c in halos:
-            c.wait_recv()
+            f_slots = to_all_blocks(field, all_f)
+        gram_sent(it - 1, before[0])
+        departure(halo_src.at[it - 1], before[1][0])
+        if it == 1:
+            departure(got.at[0, 0, 0, pl.ds(0, nz - 1)], piece_send)
+            departure(tiles.at[pl.ds(0, ny - 1)], data_send)
+            departure(rim_src, rim_send)
+            departure(got.at[0, pl.ds(0, 3), pl.ds(0, 2)], line_send)
+            departure(got.at[0, pl.ds(0, 3), pl.ds(0, 3)], later_send)
+            departure(got.at[0], partner_send)
+        halos_here(it, halo_slots)
         put_halos(it)
         stack()
         convolve()
-        if it < ITERS - 1:
-            cz = gram_along(it, cx)
         denom = correlate()
+        gram_along(it, gram_slots)
         if it == ITERS - 1:
-            d_in = to_all_blocks(denom, all_d)
-            cz = gram_along(it, cx)
-            for c in n_in + f_in:
-                c.wait_recv()
+            d_slots = to_all_blocks(denom, all_d)
+            departure(all_n.at[pl.ds(0, ny - 1)], n_slots[0])
+            arrival(all_n.at[pl.ds(0, ny - 1)], n_slots[1])
+            arrival(all_f.at[pl.ds(0, ny - 1)], f_slots[1])
             for yy in range(ny):
                 f = all_f[yy]
                 hi = f.astype(BF16)
@@ -348,24 +375,25 @@
                 fb[yy, FACTORS:2 * FACTORS, :] = (f - hi.astype(F32)).astype(BF16)
                 all_a[yy] = f * all_n[yy]
         elif it == 1:
-            n_in = to_all_blocks(num[...], all_n)
-        c1 = gram_back(it, cz)
-        off = gram_end(it, c1)
+            n_slots = to_all_blocks(num[...], all_n)
+        gram_back(it, gram_slots)
+        off = gram_end(it, gram_slots)
         if it < ITERS - 1:
             field = update(off, denom)
-        sent += halos + [c0, c1] + cx + cz
 
     off_hi = off.astype(BF16)
     off_lo = (off - off_hi.astype(F32)).astype(BF16)
     twice = jnp.concatenate([off_hi, off_hi], axis=1)
-    for c in d_in:
-        c.wait_recv()
+    departure(all_f.at[pl.ds(0, ny - 1)], f_slots[0])
+    arrival(all_d.at[pl.ds(0, ny - 1)], d_slots[1])
     for yy in range(ny):
         penalty = (jnp.dot(twice, fb[yy], preferred_element_type=F32)
                    + jnp.dot(off_lo, fb[yy, 0:FACTORS, :], preferred_element_type=F32))
         out_ref[:, own * yy:own * yy + own] = all_a[yy] / (all_d[yy] + penalty)
-    for c in sent:
-        c.wait_send()
+    departure(all_d.at[pl.ds(0, ny - 1)], d_slots[0])
+    assert count[0] == SLOTS, count[0]
+    departure(halo_src.at[ITERS - 1], halo_slots[0])
+    gram_sent(ITERS - 1, gram_slots)
 
 
 def on_device(data, motifs, loadings):
@@ -375,7 +403,6 @@
     nz = ntm // (NX * NC)
     V = pl.BlockSpec(memory_space=pltpu.VMEM)
     A = pl.BlockSpec(memory_space=pl.ANY)
-    copies = ITERS * (4 + NX * ny - 1 + nz - 1) + 160
     vm = pltpu.VMEM
     return pl.pallas_call(
         functools.partial(kernel, nz, ny, float(steps * ntm)),
@@ -412,8 +439,7 @@
             vm((ny, FACTORS, own), F32),
             vm((ny, FACTORS, own), F32),
             vm((ny, 2 * FACTORS, own), BF16),
-            pltpu.SemaphoreType.DMA((copies,)),
-            pltpu.SemaphoreType.DMA((copies,)),
+            pltpu.SemaphoreType.DMA((SLOTS,)),
             pltpu.SemaphoreType.DMA((2,)),
         ],
         compiler_params=pltpu.CompilerParams(collective_id=0, has_side_effects=True),

time: 71.9 us -> 67.9 us (0.944)
  Pallas kernels: 69.8 us -> 65.8 us
    pallas_call x1, Pallas kernels: 69.8 us -> 65.8 us  [on_device(): pl.pallas_call(functools.partial(kernel, nz, ny, float(steps * ntm)), out...]
where the time goes in v4:
time: 67.9 us; the launch traced here: 67.7 us
  Pallas kernels  65.8 us (97%)
  local copies, waits for them, and re-layouts  1.87 us (3%)
    pallas_call x1, Pallas kernels, on_device(): pl.pallas_call(functools.partial(kernel, nz, ny, float(steps * ntm)), out...  65.8 us
    unnamed x1, local copies, waits for them, and re-layouts  1.87 us

profile of v4, /device:TPU:1, one launch (start us, length us, event | category | flops | bytes accessed | tf_op | source)
XLA Modules:
  0.0 67.7 jit_solution(10864782702116196137)
XLA Ops:
  0.0 65.8 %shard_map.37 = f32[64,2048]{1,0:T(8,128)} custom-call(bf16[32,96]{1,0:T(8,128)(2,1)} %bitcast.1, bf16[96,2048]{1,0:T(8,128)(2,1)} %x_ref.1, f32[64,2048]{1,0:T(8,128)} %h_ref.1), custom_call_target="tpu_custom_call" | custom-call | tf_op jit(solution)/shard_map/pallas_call | solution.py:407
  65.8 1.9 %copy.5 = f32[64,2048]{1,0:T(8,128)} copy(f32[64,2048]{1,0:T(8,128)} %shard_map.37) | data formatting | bytes 1048576

commit v5 on v4

--- a/solution.py
+++ b/solution.py
@@ -12,7 +12,7 @@
 ITERS = 3
 LANES = 128
 HALO = LAGS
-SLOTS = 84
+SLOTS = 86
 penalty_weight = 0.2
 
 F32 = jnp.float32
@@ -27,7 +27,7 @@
 
 def kernel(nz, ny, total, m_ref, x_ref, h_ref, out_ref, src, got, wf, w_ref, tiles, h_own, rim_src, rim,
            df, hst, r, r4, q, num, fa, halo_src, halo_l, halo_r, gsrc, cbuf, part, xybuf, zbuf, gtot,
-           all_n, all_f, all_d, all_a, fb, sem, in_sem):
+           all_n, all_f, all_d, all_e, all_a, result, fb, sem, in_sem):
     blocks = m_ref.shape[1]
     own = h_ref.shape[1] // ny
     tm = lax.axis_index("tm")
@@ -327,17 +327,35 @@
         return 0
 
     lax.fori_loop(0, LAGS * FACTORS // LANES, narrow, 0)
-    num[...] = correlate()
-    convolve()
-    denom = correlate()
-    field = update(off, denom)
-
     def to_all_blocks(value, everyone_has):
         everyone_has[y] = value.T
         slots = (slot(), slot())
         for dev in along_y:
             remote(everyone_has.at[y], everyone_has.at[y], dev, *slots)
         return slots
+
+    def all_here(everyone_has, slots):
+        departure(everyone_has.at[pl.ds(0, ny - 1)], slots[0])
+        arrival(everyone_has.at[pl.ds(0, ny - 1)], slots[1])
+
+    def put_block(yy, f):
+        hi = f.astype(BF16)
+        fb[yy, 0:FACTORS, :] = hi
+        fb[yy, FACTORS:2 * FACTORS, :] = (f - hi.astype(F32)).astype(BF16)
+        all_a[yy] = f * all_n[yy]
+
+    def updated_block(yy, off, denom):
+        off_hi = off.astype(BF16)
+        off_lo = (off - off_hi.astype(F32)).astype(BF16)
+        penalty = (jnp.dot(jnp.concatenate([off_hi, off_hi], axis=1), fb[yy], preferred_element_type=F32)
+                   + jnp.dot(off_lo, fb[yy, 0:FACTORS, :], preferred_element_type=F32))
+        return all_a[yy] / (denom + penalty)
+
+    num[...] = correlate()
+    n_slots = to_all_blocks(num[...], all_n)
+    convolve()
+    denom = correlate()
+    field = update(off, denom)
 
     for it in range(1, ITERS):
         put_gram(field)
@@ -346,7 +364,7 @@
         halo_slots = send_halos(it, field)
         put_field(field)
         gram_across(it, gram_slots)
-        if it == ITERS - 1:
+        if it == ITERS - 2:
             f_slots = to_all_blocks(field, all_f)
         gram_sent(it - 1, before[0])
         departure(halo_src.at[it - 1], before[1][0])
@@ -363,37 +381,32 @@
         convolve()
         denom = correlate()
         gram_along(it, gram_slots)
+        if it == ITERS - 2:
+            d_slots = to_all_blocks(denom, all_d)
         if it == ITERS - 1:
-            d_slots = to_all_blocks(denom, all_d)
-            departure(all_n.at[pl.ds(0, ny - 1)], n_slots[0])
-            arrival(all_n.at[pl.ds(0, ny - 1)], n_slots[1])
-            arrival(all_f.at[pl.ds(0, ny - 1)], f_slots[1])
+            end_slots = to_all_blocks(denom, all_e)
+            all_here(all_n, n_slots)
+            all_here(all_f, f_slots)
+            all_here(all_d, d_slots)
             for yy in range(ny):
-                f = all_f[yy]
-                hi = f.astype(BF16)
-                fb[yy, 0:FACTORS, :] = hi
-                fb[yy, FACTORS:2 * FACTORS, :] = (f - hi.astype(F32)).astype(BF16)
-                all_a[yy] = f * all_n[yy]
-        elif it == 1:
-            n_slots = to_all_blocks(num[...], all_n)
+                put_block(yy, all_f[yy])
+                put_block(yy, updated_block(yy, off, all_d[yy]))
         gram_back(it, gram_slots)
         off = gram_end(it, gram_slots)
         if it < ITERS - 1:
             field = update(off, denom)
 
-    off_hi = off.astype(BF16)
-    off_lo = (off - off_hi.astype(F32)).astype(BF16)
-    twice = jnp.concatenate([off_hi, off_hi], axis=1)
-    departure(all_f.at[pl.ds(0, ny - 1)], f_slots[0])
-    arrival(all_d.at[pl.ds(0, ny - 1)], d_slots[1])
+    all_here(all_e, end_slots)
+    outs = []
     for yy in range(ny):
-        penalty = (jnp.dot(twice, fb[yy], preferred_element_type=F32)
-                   + jnp.dot(off_lo, fb[yy, 0:FACTORS, :], preferred_element_type=F32))
-        out_ref[:, own * yy:own * yy + own] = all_a[yy] / (all_d[yy] + penalty)
-    departure(all_d.at[pl.ds(0, ny - 1)], d_slots[0])
-    assert count[0] == SLOTS, count[0]
+        result[yy] = updated_block(yy, off, all_e[yy])
+        outs.append(pltpu.make_async_copy(result.at[yy], out_ref.at[:, pl.ds(own * yy, own)], in_sem.at[2 + yy]))
+        outs[-1].start()
     departure(halo_src.at[ITERS - 1], halo_slots[0])
     gram_sent(ITERS - 1, gram_slots)
+    for c in outs:
+        c.wait()
+    assert count[0] == SLOTS, count[0]
 
 
 def on_device(data, motifs, loadings):
@@ -408,7 +421,7 @@
         functools.partial(kernel, nz, ny, float(steps * ntm)),
         out_shape=jax.ShapeDtypeStruct((FACTORS, steps), F32),
         in_specs=[V, A, A],
-        out_specs=V,
+        out_specs=A,
         scratch_shapes=[
             vm((LAGS, LANES), BF16),
             vm((NC, ny, NX, nz, LAGS, LANES), BF16),
@@ -438,9 +451,11 @@
             vm((ny, FACTORS, own), F32),
             vm((ny, FACTORS, own), F32),
             vm((ny, FACTORS, own), F32),
+            vm((ny, FACTORS, own), F32),
+            vm((ny, FACTORS, own), F32),
             vm((ny, 2 * FACTORS, own), BF16),
             pltpu.SemaphoreType.DMA((SLOTS,)),
-            pltpu.SemaphoreType.DMA((2,)),
+            pltpu.SemaphoreType.DMA((2 + ny,)),
         ],
         compiler_params=pltpu.CompilerParams(collective_id=0, has_side_effects=True),
     )(motifs.T, data, loadings)

time: 67.9 us -> 69.4 us (1.022)
  Pallas kernels: 65.8 us -> 67.4 us
    pallas_call x1, Pallas kernels: 65.8 us -> 67.4 us  [on_device(): pl.pallas_call(functools.partial(kernel, nz, ny, float(steps * ntm)), out...]
where the time goes in v5:
time: 69.4 us; the launch traced here: 69.3 us
  Pallas kernels  67.4 us (97%)
  local copies, waits for them, and re-layouts  1.87 us (3%)
    pallas_call x1, Pallas kernels, on_device(): pl.pallas_call(functools.partial(kernel, nz, ny, float(steps * ntm)), out...  67.4 us
    unnamed x1, local copies, waits for them, and re-layouts  1.87 us

profile of v5, /device:TPU:1, one launch (start us, length us, event | category | flops | bytes accessed | tf_op | source)
XLA Modules:
  0.0 69.3 jit_solution(10800421635522072862)
XLA Ops:
  0.0 67.4 %shard_map.37 = f32[64,2048]{1,0:T(8,128)} custom-call(bf16[32,96]{1,0:T(8,128)(2,1)} %bitcast.1, bf16[96,2048]{1,0:T(8,128)(2,1)} %x_ref.1, f32[64,2048]{1,0:T(8,128)} %h_ref.1), custom_call_target="tpu_custom_call" | custom-call | tf_op jit(solution)/shard_map/pallas_call | solution.py:420
  67.4 1.9 %copy.5 = f32[64,2048]{1,0:T(8,128)} copy(f32[64,2048]{1,0:T(8,128)} %shard_map.37) | data formatting | bytes 1048576

commit v6 on v4

--- a/solution.py
+++ b/solution.py
@@ -340,10 +340,10 @@
         return slots
 
     for it in range(1, ITERS):
+        before = gram_slots, halo_slots
+        halo_slots = send_halos(it, field)
         put_gram(field)
-        before = gram_slots, halo_slots
         gram_slots = gram_start(it)
-        halo_slots = send_halos(it, field)
         put_field(field)
         gram_across(it, gram_slots)
         if it == ITERS - 1:

time: 67.9 us -> 67.5 us (level)
  no operation moved by 1% of the time
where the time goes in v6:
time: 67.5 us; the launch traced here: 67.3 us
  Pallas kernels  65.4 us (97%)
  local copies, waits for them, and re-layouts  1.87 us (3%)
    pallas_call x1, Pallas kernels, on_device(): pl.pallas_call(functools.partial(kernel, nz, ny, float(steps * ntm)), out...  65.4 us
    unnamed x1, local copies, waits for them, and re-layouts  1.87 us

profile of v6, /device:TPU:1, one launch (start us, length us, event | category | flops | bytes accessed | tf_op | source)
XLA Modules:
  0.0 67.3 jit_solution(10068110353874971614)
XLA Ops:
  0.0 65.4 %shard_map.37 = f32[64,2048]{1,0:T(8,128)} custom-call(bf16[32,96]{1,0:T(8,128)(2,1)} %bitcast.1, bf16[96,2048]{1,0:T(8,128)(2,1)} %x_ref.1, f32[64,2048]{1,0:T(8,128)} %h_ref.1), custom_call_target="tpu_custom_call" | custom-call | tf_op jit(solution)/shard_map/pallas_call | solution.py:407
  65.4 1.9 %copy.5 = f32[64,2048]{1,0:T(8,128)} copy(f32[64,2048]{1,0:T(8,128)} %shard_map.37) | data formatting | bytes 1048576
